TPU v7x, 32 devices: a whole 2x2x4 slice. The times are simulated.
32 devices in a mesh: dp: 2 (over x), ctx: 4 (over z), tp: 4 (over y, core).
Axes of the slice: x: 2, y: 2, z: 4, core: 2. Of those that a mesh axis runs over, the one named last changes fastest.
Arguments:
- tokens: bfloat16 [2, 2048, 4096], P('dp', 'ctx'), may hold values from -6 to 6
- norm_gain: float32 [4096], replicated, may hold values from 0.25 to 1.75
- zx_weight: bfloat16 [4096, 2, 8192], P(('dp', 'ctx'), None, 'tp'), may hold values from -0.09375 to 0.09375
- bc_weight: bfloat16 [4096, 2, 1024], P(('dp', 'ctx'), None, 'tp'), may hold values from -0.09375 to 0.09375
- dt_weight: bfloat16 [4096, 128], P(('dp', 'ctx'), 'tp'), may hold values from -0.09375 to 0.09375
- conv_x: float32 [5, 8192], P(None, 'tp'), may hold values from -3 to 3
- conv_bc: float32 [5, 2, 1024], P(None, None, 'tp'), may hold values from -3 to 3
- head_params: float32 [3, 128], P(None, 'tp'), may hold values from -12 to 4
- gate_gain: float32 [8192], P('tp'), may hold values from 0.25 to 1.75
- out_weight: bfloat16 [4096, 8192], P(('dp', 'ctx'), 'tp'), may hold values from -0.0625 to 0.0625
- cotangent: bfloat16 [2, 2048, 4096], P('dp', 'ctx'), may hold values from -6 to 6
Outputs:
- mixed: bfloat16 [2, 2048, 4096], P('dp', 'ctx')
- tokens_grad: float32 [2, 2048, 4096], P('dp', 'ctx')
- norm_gain_grad: float32 [4096], replicated
- zx_weight_grad: float32 [4096, 2, 8192], P(('dp', 'ctx'), None, 'tp')
- bc_weight_grad: float32 [4096, 2, 1024], P(('dp', 'ctx'), None, 'tp')
- dt_weight_grad: float32 [4096, 128], P(('dp', 'ctx'), 'tp')
- conv_x_grad: float32 [5, 8192], P(None, 'tp')
- conv_bc_grad: float32 [5, 2, 1024], P(None, None, 'tp')
- head_params_grad: float32 [3, 128], P(None, 'tp')
- gate_gain_grad: float32 [8192], P('tp')
- out_weight_grad: float32 [4096, 8192], P(('dp', 'ctx'), 'tp')
All inputs are finite; a program needn't handle non-finite values.
Results may differ from a plain program's by a relative error of at most 0.0049.
The roundings to bfloat16 on the way count: a program that leaves them out, or rounds other values in their place, can miss the bound.
Values may be sent and summed in bfloat16 or wider, within the bound.
A program may use at most 448 MiB of HBM per device.

v0:
```python
import jax
import jax.numpy as jnp
from jax import lax
from jax.sharding import PartitionSpec as P

P_SIZE = 64
N = 128
STRETCH = 256
EPS = 1e-05
HIGH = lax.Precision.HIGHEST


def shifted(value, axis, by):
    devices = lax.axis_size(axis)
    pairs = [(i, i + by) for i in range(devices) if 0 <= i + by < devices]
    return lax.ppermute(value, axis, pairs)


def carried_in(part, axis, combine, identity, reverse):
    count = lax.axis_size(axis)
    place = lax.axis_index(axis)
    ahead = count - 1 - place if reverse else place
    gathered = jax.tree.map(lambda a: lax.all_gather(a, axis), part)
    state = jax.tree.map(lambda a, e: jnp.zeros_like(a) + jnp.asarray(e, a.dtype), part, identity)

    def one(turn, state):
        source = count - 1 - turn if reverse else turn
        return combine(
            state, jax.tree.map(lambda a: lax.dynamic_index_in_dim(a, source, 0, False), gathered)
        )

    return lax.fori_loop(0, ahead, one, state)


def dot_last(left_side, right_side):
    return lax.dot_general(
        left_side, right_side, (((1,), (1,)), ((), ())), preferred_element_type=jnp.float32
    )


def dot_first(left_side, right_side):
    return lax.dot_general(
        left_side, right_side, (((0,), (0,)), ((), ())), preferred_element_type=jnp.float32
    )


def conv_silu(padded, kernel):
    tap_count = kernel.shape[0] - 1
    length = padded.shape[1] - tap_count + 1
    running = kernel[tap_count] + kernel[0] * padded[:, 0:length]
    for offset in range(1, tap_count):
        running = running + kernel[offset] * padded[:, offset : offset + length]
    return jax.nn.silu(running)


def block_step(memory, pieces, log_decay):
    x_heads, step_sizes, inject, readout = pieces
    block_len = x_heads.shape[0]
    groups = inject.shape[1]
    per_group = x_heads.shape[1] // groups
    head_dim = x_heads.shape[2]
    cumulative = jnp.cumsum(step_sizes * log_decay, axis=0)
    gap_matrix = cumulative[:, None, :] - cumulative[None, :, :]
    causal = jnp.tril(jnp.ones((block_len, block_len), jnp.float32))
    decays = jnp.exp(jnp.minimum(gap_matrix, 0.0)) * causal[:, :, None]
    scores = jnp.einsum("ign,jgn->ijg", readout, inject, precision=HIGH)
    mixing = decays.reshape(block_len, block_len, groups, per_group) * scores[:, :, :, None]
    scaled = (x_heads * step_sizes[:, :, None]).reshape(block_len, groups, per_group, head_dim)
    local_out = jnp.einsum("ijgh,jghp->ighp", mixing, scaled, precision=HIGH)
    carried = jnp.einsum("ign,ghpn->ighp", readout, memory, precision=HIGH)
    carried = carried * jnp.exp(cumulative).reshape(block_len, groups, per_group)[:, :, :, None]
    to_end = jnp.exp(cumulative[-1] - cumulative).reshape(block_len, groups, per_group)
    new_memory = memory * jnp.exp(cumulative[-1]).reshape(groups, per_group)[:, :, None, None]
    new_memory = new_memory + jnp.einsum(
        "jgn,jghp->ghpn", inject, scaled * to_end[:, :, :, None], precision=HIGH
    )
    return (new_memory, (local_out + carried).reshape(block_len, groups * per_group, head_dim))


def ssd_scan(x_heads, step_sizes, log_decay, inject, readout):
    length, head_count, head_dim = x_heads.shape
    groups, state_dim = (inject.shape[1], inject.shape[2])
    block_count = length // STRETCH
    pieces = (
        x_heads.reshape(block_count, STRETCH, head_count, head_dim),
        step_sizes.reshape(block_count, STRETCH, head_count),
        inject.reshape(block_count, STRETCH, groups, state_dim),
        readout.reshape(block_count, STRETCH, groups, state_dim),
    )
    zero_memory = jnp.zeros((groups, head_count // groups, head_dim, state_dim), jnp.float32)
    advance = jax.checkpoint(lambda memory, piece_set: block_step(memory, piece_set, log_decay))
    last_memory, outputs = lax.scan(advance, zero_memory, pieces)
    return (
        outputs.reshape(length, head_count, head_dim),
        last_memory.reshape(head_count, head_dim, state_dim),
    )


def local_states(x_flat, state_maps, raw_dt, head_params):
    seq_count, length, inner_width = x_flat.shape
    head_count = head_params.shape[1]
    groups = state_maps.shape[2] // (2 * N)
    step_sizes = jax.nn.softplus(raw_dt + head_params[0])
    log_decay = -jnp.exp(head_params[1])
    x_heads = x_flat.reshape(seq_count, length, head_count, P_SIZE)
    inject = state_maps[:, :, : groups * N].reshape(seq_count, length, groups, N)
    readout = state_maps[:, :, groups * N :].reshape(seq_count, length, groups, N)

    def single_seq(x_one, step_one, inject_one, readout_one):
        return ssd_scan(x_one, step_one, log_decay, inject_one, readout_one)

    outputs, last_memory = jax.vmap(single_seq)(x_heads, step_sizes, inject, readout)
    cumulative = jnp.cumsum(step_sizes * log_decay, axis=1)
    return (outputs, jnp.exp(cumulative[:, -1]), last_memory, cumulative)


def finish_heads(
    outputs, x_flat, state_maps, cumulative, start_state, gate_pre, head_params, gate_gain
):
    seq_count, length, inner_width = x_flat.shape
    head_count = head_params.shape[1]
    groups = state_maps.shape[2] // (2 * N)
    per_group = head_count // groups
    readout = state_maps[:, :, groups * N :].reshape(seq_count, length, groups, N)
    start_grouped = start_state.reshape(seq_count, groups, per_group, P_SIZE, N)
    carried = jnp.einsum("slgn,sghpn->slghp", readout, start_grouped, precision=HIGH)
    carried = carried * jnp.exp(cumulative).reshape(seq_count, length, groups, per_group)[..., None]
    x_heads = x_flat.reshape(seq_count, length, head_count, P_SIZE)
    total_out = (
        outputs
        + carried.reshape(seq_count, length, head_count, P_SIZE)
        + head_params[2][:, None] * x_heads
    )
    gated = total_out.reshape(seq_count, length, inner_width) * jax.nn.silu(gate_pre)
    grouped = gated.reshape(seq_count, length, groups, inner_width // groups)
    grouped = grouped * lax.rsqrt(jnp.mean(grouped * grouped, axis=-1, keepdims=True) + EPS)
    return grouped.reshape(seq_count, length, inner_width) * gate_gain


def combine_maps(earlier, later):
    return (later[0] * earlier[0], later[0][:, :, None, None] * earlier[1] + later[1])


def shards(
    tokens,
    norm_gain,
    zx_weight,
    bc_weight,
    dt_weight,
    conv_x,
    conv_bc,
    head_params,
    gate_gain,
    out_weight,
    cotangent,
):
    seq_count, length, model_width = tokens.shape
    row_count = seq_count * length
    inner_width = conv_x.shape[1]
    pair_width = bc_weight.shape[2]
    head_count = dt_weight.shape[1]
    shard_rows = dt_weight.shape[0]
    tap_count = conv_x.shape[0] - 1
    edge_rows = tap_count - 1
    hidden = tokens.astype(jnp.float32)
    rscale = lax.rsqrt(jnp.mean(hidden * hidden, axis=-1, keepdims=True) + EPS)
    normed = (hidden * rscale * norm_gain).astype(jnp.bfloat16).reshape(row_count, model_width)
    pieces = (
        lax.all_gather(zx_weight, ("dp", "ctx"), axis=0, tiled=True),
        lax.all_gather(bc_weight, ("dp", "ctx"), axis=0, tiled=True),
        lax.all_gather(dt_weight, ("dp", "ctx"), axis=0, tiled=True),
    )
    row_span = pieces[0].shape[0]
    columns = normed
    proj_zx = jnp.dot(
        columns, pieces[0].reshape(row_span, 2 * inner_width), preferred_element_type=jnp.float32
    )
    proj_bc = jnp.dot(
        columns, pieces[1].reshape(row_span, 2 * pair_width), preferred_element_type=jnp.float32
    )
    raw_dt = jnp.dot(columns, pieces[2], preferred_element_type=jnp.float32)
    gate_pre = proj_zx[:, :inner_width].reshape(seq_count, length, inner_width)
    conv_input = jnp.concatenate([proj_zx[:, inner_width:], proj_bc], axis=1).astype(jnp.bfloat16)
    conv_input = conv_input.reshape(seq_count, length, inner_width + 2 * pair_width)
    before_rows = shifted(conv_input[:, length - edge_rows :], "ctx", 1)
    padded = jnp.concatenate([before_rows, conv_input], axis=1).astype(jnp.float32)
    kernel = jnp.concatenate([conv_x, conv_bc.reshape(tap_count + 1, 2 * pair_width)], axis=1)
    conv_out, conv_back = jax.vjp(conv_silu, padded, kernel)
    conv_low = lax.optimization_barrier(conv_out.astype(jnp.bfloat16)).astype(jnp.float32)
    x_flat = conv_low[:, :, :inner_width]
    state_maps = conv_low[:, :, inner_width:]
    step_raw = raw_dt.reshape(seq_count, length, head_count)
    summary, states_back = jax.vjp(local_states, x_flat, state_maps, step_raw, head_params)
    outputs, span_decay, last_memory, cumulative = summary
    identity_pair = (jnp.ones_like(span_decay), jnp.zeros_like(last_memory))
    start_state = carried_in((span_decay, last_memory), "ctx", combine_maps, identity_pair, False)[
        1
    ]
    gated_full, finish_back = jax.vjp(
        finish_heads,
        outputs,
        x_flat,
        state_maps,
        cumulative,
        start_state,
        gate_pre,
        head_params,
        gate_gain,
    )
    gated_norm = gated_full.astype(jnp.bfloat16).reshape(row_count, inner_width)
    branch_out = dot_last(gated_norm, lax.all_gather(out_weight, ("dp", "ctx"), axis=0, tiled=True))
    flat_hidden = hidden.reshape(row_count, model_width)
    branch_total = lax.psum(branch_out, "tp")
    mixed = (flat_hidden + branch_total).astype(jnp.bfloat16)
    mixed = mixed.reshape(seq_count, length, model_width)
    flat_cot = cotangent.reshape(row_count, model_width)
    columns = flat_cot
    grad_gated = jnp.dot(
        columns,
        lax.all_gather(out_weight, ("dp", "ctx"), axis=0, tiled=True),
        preferred_element_type=jnp.float32,
    )
    (
        grad_outputs,
        grad_x_one,
        grad_maps_one,
        grad_cumul,
        grad_start,
        grad_gate,
        grad_head_one,
        gate_gain_grad,
    ) = finish_back(grad_gated.reshape(seq_count, length, inner_width))
    later_grad = carried_in((span_decay, grad_start), "ctx", combine_maps, identity_pair, True)[1]
    grad_decay = jnp.sum(later_grad * start_state, axis=(2, 3))
    grad_x_two, grad_maps_two, grad_step, grad_head_two = states_back(
        (grad_outputs, grad_decay, later_grad, grad_cumul)
    )
    grad_conv_out = jnp.concatenate(
        [grad_x_one + grad_x_two, grad_maps_one + grad_maps_two], axis=2
    )
    grad_padded, grad_kernel = conv_back(grad_conv_out)
    returned_rows = shifted(grad_padded[:, :edge_rows], "ctx", -1)
    grad_input = grad_padded[:, edge_rows:]
    grad_input = jnp.concatenate(
        [grad_input[:, : length - edge_rows], grad_input[:, length - edge_rows :] + returned_rows],
        axis=1,
    )
    grad_input = grad_input.reshape(row_count, inner_width + 2 * pair_width)
    grad_zx = jnp.concatenate(
        [grad_gate.reshape(row_count, inner_width), grad_input[:, :inner_width]], axis=1
    ).astype(jnp.bfloat16)
    grad_bc = grad_input[:, inner_width:].astype(jnp.bfloat16)
    grad_dt = grad_step.reshape(row_count, head_count).astype(jnp.bfloat16)
    pieces = (
        lax.all_gather(zx_weight, ("dp", "ctx"), axis=0, tiled=True),
        lax.all_gather(bc_weight, ("dp", "ctx"), axis=0, tiled=True),
        lax.all_gather(dt_weight, ("dp", "ctx"), axis=0, tiled=True),
    )
    row_span = pieces[0].shape[0]
    contrib = dot_last(grad_zx, pieces[0].reshape(row_span, 2 * inner_width))
    contrib = contrib + dot_last(grad_bc, pieces[1].reshape(row_span, 2 * pair_width))
    contrib = contrib + dot_last(grad_dt, pieces[2])
    grad_normed = contrib
    grad_normed = lax.psum(grad_normed, "tp")
    flat_scale = rscale.reshape(row_count, 1)
    grad_hat = grad_normed * norm_gain
    norm_gain_grad = jnp.sum(grad_normed * flat_hidden * flat_scale, axis=0)
    grad_hidden = flat_scale * grad_hat - flat_hidden * (
        flat_scale * flat_scale * flat_scale
    ) * jnp.mean(grad_hat * flat_hidden, axis=1, keepdims=True)
    tokens_grad = (flat_cot.astype(jnp.float32) + grad_hidden).reshape(
        seq_count, length, model_width
    )
    zx_end = 2 * inner_width
    bc_end = zx_end + 2 * pair_width
    dt_end = bc_end + head_count
    weight_sum = lax.psum_scatter(
        jnp.concatenate(
            [
                jnp.concatenate(
                    [
                        dot_first(normed, grad_zx),
                        dot_first(normed, grad_bc),
                        dot_first(normed, grad_dt),
                    ],
                    axis=1,
                ),
                dot_first(flat_cot, gated_norm),
            ],
            axis=1,
        ),
        ("dp", "ctx"),
        scatter_dimension=0,
        tiled=True,
    )
    out_weight_grad = weight_sum[:, dt_end:]
    zx_weight_grad = weight_sum[:, :zx_end].reshape(shard_rows, 2, inner_width)
    bc_weight_grad = weight_sum[:, zx_end:bc_end].reshape(shard_rows, 2, pair_width)
    dt_weight_grad = weight_sum[:, bc_end:dt_end]
    small_sums = lax.psum(
        (
            norm_gain_grad,
            grad_kernel[:, :inner_width],
            grad_kernel[:, inner_width:].reshape(tap_count + 1, 2, pair_width),
            grad_head_one + grad_head_two,
            gate_gain_grad,
        ),
        ("dp", "ctx"),
    )
    return (
        mixed,
        tokens_grad,
        small_sums[0],
        zx_weight_grad,
        bc_weight_grad,
        dt_weight_grad,
        small_sums[1],
        small_sums[2],
        small_sums[3],
        small_sums[4],
        out_weight_grad,
    )


def solution(mesh):
    return jax.shard_map(
        shards,
        mesh=mesh,
        in_specs=(
            P("dp", "ctx", None),
            P(),
            P(("dp", "ctx"), None, "tp"),
            P(("dp", "ctx"), None, "tp"),
            P(("dp", "ctx"), "tp"),
            P(None, "tp"),
            P(None, None, "tp"),
            P(None, "tp"),
            P("tp"),
            P(("dp", "ctx"), "tp"),
            P("dp", "ctx", None),
        ),
        out_specs=(
            P("dp", "ctx", None),
            P("dp", "ctx", None),
            P(),
            P(("dp", "ctx"), None, "tp"),
            P(("dp", "ctx"), None, "tp"),
            P(("dp", "ctx"), "tp"),
            P(None, "tp"),
            P(None, None, "tp"),
            P(None, "tp"),
            P("tp"),
            P(("dp", "ctx"), "tp"),
        ),
        check_vma=False,
    )
```

profile of v0, /device:TPU:0, one launch (start us, length us, event | category | flops | bytes accessed | tf_op | source)
XLA Modules:
  0.0 3656.5 jit_solution(2228593473752931483)
XLA Ops:
  8.8 34.3 all_gather.28
  50.5 38.7 %all-gather.8.cloned.1.call-done = bf16[4096,2,256]{2,1,0:T(2,128)(2,1)} async-done(((bf16[512,2,256]{2,1,0:T(2,128)(2,1)}), bf16[4096,2,256]{2,1,0:T(2,128)(2,1)}) %all-gather.8.cloned.1.call-update) | async-done | bytes 4194320 | tf_op jit(solution)/shard_map/all_gather | solution.py:170
  96.7 630.1 %all-gather.6.cloned.1.call-done = bf16[4096,2,2048]{2,1,0:T(2,128)(2,1)} async-done(((bf16[512,2,2048]{2,1,0:T(2,128)(2,1)}), bf16[4096,2,2048]{2,1,0:T(2,128)(2,1)}) %all-gather.6.cloned.1.call-update) | async-done | bytes 33554448 | tf_op jit(solution)/shard_map/all_gather | solution.py:169
  726.8 23.2 copy.526
  750.0 22.8 fusion.190
  789.2 7.8 reshape.1529
  797.0 7.8 copy.416
  807.3 44.8 %while.68 = (s32[]{:T(128)}, f32[1,2,16,64,128]{4,3,2,1,0:T(8,128)S(1)}, f32[2,1,256,32,64]{2,4,3,1,0:T(8,128)}, f32[2,1,2,16,64,128]{5,4,3,2,1,0:T(8,128)}, f32...) while((s32[]{:T(128)}, ...), condition=%wide.region_4.5_spmd.clone, body=%wide.region_1.4_spmd.clone.sunk | while | flops 3436068864 | bytes 62821912 | solution.py:92
  813.4 9.3 fusion.272
  835.6 9.3 fusion.272
  859.1 12.9 all_gather.31
  875.1 9.1 copy.463
  884.3 7.8 reshape.1526
  892.1 44.2 %all-gather.10.cloned.1.call-done = f32[4,1,32,64,128]{4,3,2,1,0:T(8,128)} async-done(((f32[1,1,32,64,128]{4,3,2,1,0:T(8,128)}), f32[4,1,32,64,128]{4,3,2,1,0:T(8,128)}) %all-gather.10.cloned.1.call-update) | async-done | bytes 4194320 | tf_op jit(solution)/shard_map/all_gather | solution.py:23
  941.6 5.6 copy.426
  947.2 217.2 %all-gather.12.cloned.1.call-done = bf16[4096,2048]{1,0:T(8,128)(2,1)} async-done(((bf16[512,2048]{1,0:T(8,128)(2,1)}), bf16[4096,2048]{1,0:T(8,128)(2,1)}) %all-gather.12.cloned.1.call-update) | async-done | bytes 16777232 | tf_op jit(solution)/shard_map/all_gather | solution.py:211
  1164.4 21.4 multiply_multiply_fusion
  1185.8 6.6 mul.956
  1195.9 6.6 mul.945
  1202.4 6.7 mul.946
  1224.5 8.0 fusion.144
  1248.0 8.0 reshape.1527
  1262.2 7.9 copy.438
  1270.1 12.2 multiply_reduce_fusion.6
  1282.3 15.4 convolution_bitcast_fusion.3
  1297.7 14.9 fusion.201
  1312.6 9.6 all-gather.14.cloned.1.call-done
  1338.5 164.0 %while.69 = (s32[]{:T(128)}, f32[32]{0:T(128)}, f32[1,2,16,64,128]{4,3,2,1,0:T(8,128)S(1)}, f32[2,1,256,32,64]{2,4,3,1,0:T(8,128)}, f32[2,1,256,32]{2,0,3,1:T(2,...) while((s32[]{:T(128)}, f32[32]{0:T(128)}, ...), condition=%wide.region_28.29_spmd.clone, body=%wide.region_14.28_spmd.clone.sunk | while | flops 7901773824 | bytes 110699288 | solution.py:92
  1369.3 14.5 fusion.297
  1392.1 7.2 bitcast_add_fusion.14
  1450.7 14.5 fusion.297
  1473.5 7.2 bitcast_add_fusion.14
  1510.6 9.1 copy.470
  1519.7 7.9 reshape.1528
  1532.4 8.6 multiply_reduce_fusion.5
  1541.0 10.6 broadcast_multiply_fusion.2
  1571.0 22.9 fusion.158
  1593.9 10.4 add_add_fusion
  1605.0 30.2 fusion.157
  1635.2 7.0 fusion.164
  1642.3 74.9 %pad_maximum_fusion = f32[4096,6688]{0,1:T(8,128)} fusion(f32[4096,2048]{0,1:T(8,128)} %convolution_bitcast_fusion.3, f32[4096,32]{0,1:T(8,128)S(1)} %fusion.177, f32[4096,512]{0,1:T(8,128)} %fusion.164, f32[4096,4096]{0,1:T(8,128)} %fusion.157), kind=kLoop, calls=%fused_computation.166 | loop fusion | flops 82182144 | bytes 219152384 | tf_op jit(solution)/shard_map/concatenate | solution.py:278
  1720.8 170.7 %all-reduce.25.cloned.1.call-done = (f32[512,4096]{1,0:T(8,128)}, f32[512,4096]{1,0:T(8,128)}) async-done(((f32[512,4096]{1,0:T(8,128)}, f32[512,4096]{1,0:T(8,128)}), (f32[512,4096]{1,0:T(8,128)}, f32[512,4096]{1,0:T(8,128)})) %all-reduce.25.cloned.1.call-update) | async-done | bytes 16777232 | tf_op jit(solution)/shard_map/psum | solution.py:213
  1891.5 7.4 fusion.133
  1898.9 15.8 fusion.130
  1914.8 1653.0 %reduce-scatter.2.cloned.1.call-done = f32[512,6688]{0,1:T(8,128)} async-done(((f32[4096,6688]{0,1:T(8,128)}), f32[512,6688]{0,1:T(8,128)}) %reduce-scatter.2.cloned.1.call-update) | async-done | bytes 13697040 | tf_op jit(solution)/shard_map/reduce_scatter | solution.py:277
  3570.4 7.6 slice.239
  3578.0 13.3 copy.448
  3602.6 40.1 %all-reduce.23.cloned.1.call-done = (f32[4096]{0:T(1024)}, f32[5,2048]{1,0:T(8,128)}, f32[5,2,256]{2,1,0:T(2,128)}, f32[3,32]{1,0:T(4,128)}, f32[2048]{0:T(1024)}) async-done(((f32[4096]{0:T(1024)}, f32[5,2048]{1,0:T(8,128)}, f32[5,2,256]{2,1,0:T(2,128)}, f32[3,32]{1,0:T(4,128)}, f32[2048]{0:T(1024)}), (f32[4096]{0:T(1024)}, f32[5,2048]{1,0:T(8,128)}, f32[5,2,256]{2,1,0:T(2,128)}, f32[3,32]{1,0:T(4,128)}, ...) | async-done | bytes 76176 | tf_op jit(solution)/shard_map/psum | solution.py:300
  (501 shorter events, 313.5 us)
Async XLA Ops:
  7.2 35.9 copy-start.77
  7.2 82.0 %all-gather.8.cloned.1.call-start = ((), (), s32[]{:S(2)}) async-start(), calls=%async_computation.2 | async-start | bytes 4718592 | tf_op jit(solution)/shard_map/all_gather | solution.py:170
  7.9 39.5 %copy-start.56 = (f32[4096]{0:T(1024)S(1)}, f32[4096]{0:T(1024)}, u32[]{:S(2)}) copy-start(f32[4096]{0:T(1024)} %param.20) | copy-start | bytes 49156
  8.0 718.8 %all-gather.6.cloned.1.call-start = ((), (), s32[]{:S(2)}) async-start(), calls=%async_computation.1 | async-start | bytes 37748736 | tf_op jit(solution)/shard_map/all_gather | solution.py:169
  8.7 927.6 %all-gather.10.cloned.1.call-start = ((), (), s32[]{:S(2)}) async-start(), calls=%async_computation.3 | async-start | bytes 5242880 | tf_op jit(solution)/shard_map/all_gather | solution.py:23
  8.8 38.7 %copy-start.19 = (bf16[1,512,4096]{2,1,0:T(8,128)(2,1)S(1)}, bf16[1,512,4096]{2,1,0:T(8,128)(2,1)}, u32[]{:S(2)}) copy-start(bf16[1,512,4096]{2,1,0:T(8,128)(2,1)} %param.19) | copy-start | bytes 12582916
  47.4 702.5 %copy-start.70 = (f32[512]{0:T(512)}, f32[512]{0:T(512)S(1)}, u32[]{:S(2)}) copy-start(f32[512]{0:T(512)S(1)} %get-tuple-element.1004) | copy-start | bytes 6148
  50.5 728.6 %copy-start.48 = (f32[2560]{0:T(1024)}, f32[2560]{0:T(1024)S(1)}, u32[]{:S(2)}) copy-start(f32[2560]{0:T(1024)S(1)} %get-tuple-element.881) | copy-start | bytes 30724
  50.5 728.6 %copy-start.50 = (f32[2560]{0:T(1024)}, f32[2560]{0:T(1024)S(1)}, u32[]{:S(2)}) copy-start(f32[2560]{0:T(1024)S(1)} %get-tuple-element.882) | copy-start | bytes 30724
  50.5 728.6 %copy-start.52 = (f32[2560]{0:T(1024)}, f32[2560]{0:T(1024)S(1)}, u32[]{:S(2)}) copy-start(f32[2560]{0:T(1024)S(1)} %get-tuple-element.883) | copy-start | bytes 30724
  50.5 728.6 %copy-start.54 = (f32[2560]{0:T(1024)}, f32[2560]{0:T(1024)S(1)}, u32[]{:S(2)}) copy-start(f32[2560]{0:T(1024)S(1)} %get-tuple-element.884) | copy-start | bytes 30724
  773.5 4.9 collective-permute-start
  853.3 18.7 copy-start.13
  853.3 311.1 %all-gather.12.cloned.1.call-start = ((), (), s32[]{:S(2)}) async-start(), calls=%async_computation.4 | async-start | bytes 18874368 | tf_op jit(solution)/shard_map/all_gather | solution.py:211
  853.9 468.3 %all-gather.14.cloned.1.call-start = ((), (), s32[]{:S(2)}) async-start(), calls=%async_computation.5 | async-start | bytes 5242880 | tf_op jit(solution)/shard_map/all_gather | solution.py:23
  854.1 310.3 %copy-start.68 = (f32[2048]{0:T(1024)}, f32[2048]{0:T(1024)S(1)}, u32[]{:S(2)}) copy-start(f32[2048]{0:T(1024)S(1)} %mul.940) | copy-start | bytes 24580
  941.6 222.8 %copy-start.65 = (f32[2048]{0:T(1024)S(1)}, f32[2048]{0:T(1024)}, u32[]{:S(2)}) copy-start(f32[2048]{0:T(1024)} %param.27) | copy-start | bytes 24580
  1214.1 10.3 slice-start.2
  1216.2 8.3 copy-start.17
  1216.2 8.3 slice-start.3
  1224.4 8.0 copy-start.18
  1243.1 648.4 %all-reduce.25.cloned.1.call-start = ((), (), s32[]{:S(2)}) async-start(), calls=%async_computation.8 | async-start | bytes 33554432 | tf_op jit(solution)/shard_map/psum | solution.py:213
  1270.1 12.2 copy-start.33
  1332.3 6.2 copy-start.46
  1369.3 14.5 copy-start.6
  1369.3 14.5 copy-start.22
  1369.3 15.7 copy-start.40
  1389.5 9.8 copy-start.31
  1392.1 8.5 copy-start
  1450.7 14.5 copy-start.6
  1450.7 14.5 copy-start.22
  1450.7 15.7 copy-start.40
  1470.9 9.8 copy-start.31
  1473.5 8.5 copy-start
  1519.7 7.9 copy-start.69
  1519.7 12.6 slice-start
  1532.4 8.6 copy-start.49
  1532.4 8.6 copy-start.51
  1532.4 8.6 copy-start.53
  1532.4 8.6 copy-start.55
  1551.6 7.2 copy-start.10
  1552.7 9.5 collective-permute-start.1
  1562.5 8.5 copy-start.29
  1571.0 22.9 copy-start.44
  1604.3 1963.4 %reduce-scatter.2.cloned.1.call-start = ((), (), s32[]{:S(2)}) async-start(), calls=%async_computation.6 | async-start | bytes 123273216 | tf_op jit(solution)/shard_map/reduce_scatter | solution.py:277
  1605.0 30.2 copy-start.21
  1717.3 1925.5 %all-reduce.23.cloned.1.call-start = ((), (), s32[]{:S(2)}) async-start(), calls=%async_computation.7 | async-start | bytes 204800 | tf_op jit(solution)/shard_map/psum | solution.py:300
  1891.5 7.4 copy-start.74
  (63 other events, 178.0 us)
Sparse Core Ops, SparseCore 0:
  10.2 79.0 all-gather.7
  90.8 635.9 all-gather.5
  853.4 82.7 all-gather.9
  938.2 226.1 all-gather.11
  1243.2 78.9 all-gather.13
  1604.5 287.0 all-reduce.24
  1895.4 1672.3 reduce-scatter.1
  3573.3 69.3 all-reduce.22
where the time goes:
time: 3670 us; the launch traced here: 3660 us
  waiting for transfers between devices  2810 us (77%)
  matrix products  286 us (8%)
  local copies, waits for them, and re-layouts  263 us (7%)
  other arithmetic  231 us (6%)
  blocking collectives  47.2 us (1%)
    reduce_scatter x1, waiting for transfers between devices, shards(): lax.psum_scatter(jnp.concatenate([jnp.concatenate([dot_first(normed, grad...  1650 us
    all_gather x1, waiting for transfers between devices, shards(): lax.all_gather(zx_weight, ('dp', 'ctx'), axis=0, tiled=True)  630 us
    all_gather x1, waiting for transfers between devices, shards(): lax.all_gather(out_weight, ('dp', 'ctx'), axis=0, tiled=True)  217 us
    psum x1, waiting for transfers between devices, shards(): branch_total = lax.psum(branch_out, 'tp')  171 us
    unnamed x144, local copies, waits for them, and re-layouts  87.5 us
    concatenate x1, other arithmetic, shards(): jnp.concatenate([jnp.concatenate([dot_first(normed, grad_zx), dot_first(n...  74.9 us
  transfers between devices with their start and end apart: 10, of which 9 were waited for; matrix products, arithmetic and copies ran while one was open for 8% of the time, Pallas kernels for 0%

commit v1 on v0

--- a/solution.py
+++ b/solution.py
@@ -8,6 +8,27 @@
 STRETCH = 256
 EPS = 1e-05
 HIGH = lax.Precision.HIGHEST
+
+
+def ring_gather(value, axis, dim):
+    count, place, rows = (lax.axis_size(axis), lax.axis_index(axis), value.shape[dim])
+    right = [(i, (i + 1) % count) for i in range(count)]
+    left = [(i, (i - 1) % count) for i in range(count)]
+    filled = jnp.zeros((*value.shape[:dim], count * rows, *value.shape[dim + 1 :]), value.dtype)
+    filled = lax.dynamic_update_slice_in_dim(filled, value, place * rows, axis=dim)
+    from_left = from_right = value
+    half = count // 2
+    for step in range(1, half + 1):
+        from_left = lax.ppermute(from_left, axis, right)
+        filled = lax.dynamic_update_slice_in_dim(
+            filled, from_left, (place - step) % count * rows, axis=dim
+        )
+        if step < count - half:
+            from_right = lax.ppermute(from_right, axis, left)
+            filled = lax.dynamic_update_slice_in_dim(
+                filled, from_right, (place + step) % count * rows, axis=dim
+            )
+    return filled
 
 
 def shifted(value, axis, by):
@@ -208,7 +229,7 @@
         gate_gain,
     )
     gated_norm = gated_full.astype(jnp.bfloat16).reshape(row_count, inner_width)
-    branch_out = dot_last(gated_norm, lax.all_gather(out_weight, ("dp", "ctx"), axis=0, tiled=True))
+    branch_out = dot_last(gated_norm, ring_gather(out_weight, ("dp", "ctx"), 0))
     flat_hidden = hidden.reshape(row_count, model_width)
     branch_total = lax.psum(branch_out, "tp")
     mixed = (flat_hidden + branch_total).astype(jnp.bfloat16)

time: 3670 us -> 4010 us (1.093)
  starting transfers between devices: 5.65 us -> 250 us
  blocking collectives: 47.2 us -> 119 us
    ppermute x0 -> x7, waiting for transfers between devices: none -> 260 us  [the longest x4 249 us: ring_gather(): from_left = lax.ppermute(from_left, axis, right)]
    ppermute x0 -> x7, starting transfers between devices: none -> 244 us  [the longest x4 239 us: ring_gather(): from_left = lax.ppermute(from_left, axis, right)]
    all_gather x1, waiting for transfers between devices: 217 us -> 0.01 us  [shards(): lax.all_gather(out_weight, ('dp', 'ctx'), axis=0, tiled=True)]
    all_gather x1, blocking collectives: 12.9 us -> 84.5 us  [carried_in(): gathered = jax.tree.map(lambda a: lax.all_gather(a, axis), part)]
    all_gather x2, waiting for transfers between devices: 53.8 us -> 13.5 us  [carried_in(): gathered = jax.tree.map(lambda a: lax.all_gather(a, axis), part)]
    unnamed x144 -> x146, local copies, waits for them, and re-layouts: 87.5 us -> 89.5 us
  transfers between devices with their start and end apart: 10 -> 17, of which waited for: 9 -> 12; matrix products, arithmetic and copies ran while one was open for 8% -> 8% of each run, Pallas kernels for 0% -> 0%
where the time goes in v1:
time: 4010 us; the launch traced here: 4000 us
  waiting for transfers between devices  2810 us (70%)
  local copies, waits for them, and re-layouts  287 us (7%)
  matrix products  286 us (7%)
  starting transfers between devices  250 us (6%)
  other arithmetic  232 us (6%)
  blocking collectives  119 us (3%)
    reduce_scatter x1, waiting for transfers between devices, shards(): lax.psum_scatter(jnp.concatenate([jnp.concatenate([dot_first(normed, grad...  1650 us
    all_gather x1, waiting for transfers between devices, shards(): lax.all_gather(zx_weight, ('dp', 'ctx'), axis=0, tiled=True)  630 us
    ppermute x4, waiting for transfers between devices, ring_gather(): from_left = lax.ppermute(from_left, axis, right)  249 us
    ppermute x4, starting transfers between devices, ring_gather(): from_left = lax.ppermute(from_left, axis, right)  239 us
    psum x1, waiting for transfers between devices, shards(): branch_total = lax.psum(branch_out, 'tp')  170 us
    unnamed x146, local copies, waits for them, and re-layouts  89.5 us
    all_gather x1, blocking collectives, carried_in(): gathered = jax.tree.map(lambda a: lax.all_gather(a, axis), part)  84.5 us
  transfers between devices with their start and end apart: 17, of which 12 were waited for; matrix products, arithmetic and copies ran while one was open for 8% of the time, Pallas kernels for 0%

profile of v1, /device:TPU:0, one launch (start us, length us, event | category | flops | bytes accessed | tf_op | source)
XLA Modules:
  0.0 3998.2 jit_solution(12803940412213021302)
XLA Ops:
  8.8 34.3 all_gather.27
  50.5 38.7 all-gather.8.cloned.1.call-done
  96.7 630.0 %all-gather.6.cloned.1.call-done = bf16[4096,2,2048]{2,1,0:T(2,128)(2,1)} async-done(((bf16[512,2,2048]{2,1,0:T(2,128)(2,1)}), bf16[4096,2,2048]{2,1,0:T(2,128)(2,1)}) %all-gather.6.cloned.1.call-update) | async-done | bytes 33554448 | tf_op jit(solution)/shard_map/all_gather | solution.py:190
  726.8 23.2 copy.526
  750.0 22.8 fusion.190
  787.6 7.8 reshape.1529
  795.4 7.8 copy.416
  805.7 44.8 %while.68 = (s32[]{:T(128)}, f32[1,2,16,64,128]{4,3,2,1,0:T(8,128)S(1)}, f32[2,1,256,32,64]{2,4,3,1,0:T(8,128)}, f32[2,1,2,16,64,128]{5,4,3,2,1,0:T(8,128)}, f32...) while((s32[]{:T(128)}, ...), condition=%wide.region_4.5_spmd.clone, body=%wide.region_1.4_spmd.clone.sunk | while | flops 3436068864 | bytes 62821912 | solution.py:113
  811.8 9.3 fusion.272
  834.0 9.3 fusion.272
  857.3 83.2 %collective-permute-done.1 = bf16[512,2048]{1,0:T(8,128)(2,1)S(1)} collective-permute-done((bf16[512,2048]{1,0:T(8,128)(2,1)}, bf16[512,2048]{1,0:T(8,128)(2,1)S(1)}, u32[]{:S(2)}, u32[]{:S(2)}) %collective-permute-start.1) | collective-permute-done | bytes 2097184 | tf_op jit(solution)/shard_map/ppermute | solution.py:22
  941.8 72.0 %collective-permute-start.3 = (bf16[512,2048]{1,0:T(8,128)(2,1)S(1)}, bf16[512,2048]{1,0:T(8,128)(2,1)}, u32[]{:S(2)}, u32[]{:S(2)}) collective-permute-start(bf16[512,2048]{1,0:T(8,128)(2,1)S(1)} %collective-permute-done.1), channel_id=1, source_target_pairs={{0,4},{4,8},{8,12},{12,16},{16,20},{20,24},{24,28},{28,0},{1,5},{5... | collective-permute-start | bytes 6291464 | tf_op jit(solution)/shard_map/ppermute | solution.py:22
  1018.8 85.2 %collective-permute-done.3 = bf16[512,2048]{1,0:T(8,128)(2,1)} collective-permute-done((bf16[512,2048]{1,0:T(8,128)(2,1)S(1)}, bf16[512,2048]{1,0:T(8,128)(2,1)}, u32[]{:S(2)}, u32[]{:S(2)}) %collective-permute-start.3) | collective-permute-done | bytes 2097184 | tf_op jit(solution)/shard_map/ppermute | solution.py:22
  1104.1 72.7 %collective-permute-start.5 = (bf16[512,2048]{1,0:T(8,128)(2,1)}, bf16[512,2048]{1,0:T(8,128)(2,1)}, u32[]{:S(2)}, u32[]{:S(2)}) collective-permute-start(bf16[512,2048]{1,0:T(8,128)(2,1)} %collective-permute-done.3), channel_id=1, source_target_pairs={{0,4},{4,8},{8,12},{12,16},{16,20},{20,24},{24,28},{28,0},{1,5},{5... | collective-permute-start | bytes 6291464 | tf_op jit(solution)/shard_map/ppermute | solution.py:22
  1179.3 9.5 collective-permute-done.4
  1189.0 80.1 %collective-permute-done.5 = bf16[512,2048]{1,0:T(8,128)(2,1)} collective-permute-done((bf16[512,2048]{1,0:T(8,128)(2,1)}, bf16[512,2048]{1,0:T(8,128)(2,1)}, u32[]{:S(2)}, u32[]{:S(2)}) %collective-permute-start.5) | collective-permute-done | bytes 2097184 | tf_op jit(solution)/shard_map/ppermute | solution.py:22
  1269.0 91.2 %collective-permute-start.7 = (bf16[512,2048]{1,0:T(8,128)(2,1)}, bf16[512,2048]{1,0:T(8,128)(2,1)S(1)}, u32[]{:S(2)}, u32[]{:S(2)}) collective-permute-start(bf16[512,2048]{1,0:T(8,128)(2,1)} %collective-permute-done.5), channel_id=1, source_target_pairs={{0,4},{4,8},{8,12},{12,16},{16,20},{20,24},{24,28},{28,0},{1,5},{5... | collective-permute-start | bytes 6291464 | tf_op jit(solution)/shard_map/ppermute | solution.py:22
  1360.2 84.5 %all_gather.30 = f32[4,1,32]{2,1,0:T(1,128)S(1)} all-gather(f32[1,1,32]{2,1,0:T(1,128)S(1)} %slice_exponential_fusion.1), channel_id=1, replica_groups=mesh['dp'=2,'ctx'=4,'tp'=4] {'ctx'}, dimensions={0}, use_global_device_ids=true | all-gather | bytes 640 | tf_op jit(solution)/shard_map/all_gather | solution.py:44
  1475.3 9.1 copy.463
  1484.4 7.8 reshape.1526
  1503.0 21.4 multiply_multiply_fusion
  1563.1 8.0 fusion.144
  1586.6 8.0 reshape.1527
  1601.4 7.8 copy.438
  1609.2 12.2 multiply_reduce_fusion.6
  1621.4 15.4 convolution_bitcast_fusion.3
  1636.9 15.0 fusion.201
  1651.8 13.5 all-gather.14.cloned.1.call-done
  1682.4 161.7 %while.69 = (s32[]{:T(128)}, f32[32]{0:T(128)}, f32[1,2,16,64,128]{4,3,2,1,0:T(8,128)S(1)}, f32[2,1,256,32,64]{2,4,3,1,0:T(8,128)}, f32[2,1,256,32]{2,0,3,1:T(2,...) while((s32[]{:T(128)}, f32[32]{0:T(128)}, ...), condition=%wide.region_28.29_spmd.clone, body=%wide.region_14.28_spmd.clone.sunk | while | flops 7901773824 | bytes 114893656 | solution.py:113
  1712.3 14.5 fusion.297
  1735.0 7.2 bitcast_add_fusion.14
  1792.5 14.5 fusion.297
  1815.2 7.2 bitcast_add_fusion.14
  1852.3 9.1 copy.470
  1861.4 7.9 reshape.1528
  1874.1 8.6 multiply_reduce_fusion.5
  1882.7 10.6 broadcast_multiply_fusion.2
  1912.7 22.9 fusion.158
  1935.6 10.4 add_add_fusion
  1946.7 30.2 fusion.157
  1984.0 75.6 %pad_maximum_fusion = f32[4096,6688]{0,1:T(8,128)} fusion(f32[4096,2048]{0,1:T(8,128)} %convolution_bitcast_fusion.3, f32[4096,32]{0,1:T(8,128)S(1)} %fusion.177, f32[4096,512]{0,1:T(8,128)} %fusion.164, f32[4096,4096]{0,1:T(8,128)} %fusion.157), kind=kLoop, calls=%fused_computation.166 | loop fusion | flops 82182144 | bytes 219152384 | tf_op jit(solution)/shard_map/concatenate | solution.py:299
  2063.2 170.0 %all-reduce.25.cloned.1.call-done = (f32[512,4096]{1,0:T(8,128)}, f32[512,4096]{1,0:T(8,128)}) async-done(((f32[512,4096]{1,0:T(8,128)}, f32[512,4096]{1,0:T(8,128)}), (f32[512,4096]{1,0:T(8,128)}, f32[512,4096]{1,0:T(8,128)})) %all-reduce.25.cloned.1.call-update) | async-done | bytes 16777232 | tf_op jit(solution)/shard_map/psum | solution.py:234
  2233.2 7.4 fusion.133
  2240.6 15.8 fusion.130
  2256.5 1653.0 %reduce-scatter.2.cloned.1.call-done = f32[512,6688]{0,1:T(8,128)} async-done(((f32[4096,6688]{0,1:T(8,128)}), f32[512,6688]{0,1:T(8,128)}) %reduce-scatter.2.cloned.1.call-update) | async-done | bytes 13697040 | tf_op jit(solution)/shard_map/reduce_scatter | solution.py:298
  3912.1 7.6 slice.239
  3919.7 13.3 copy.448
  3944.3 40.1 %all-reduce.23.cloned.1.call-done = (f32[4096]{0:T(1024)}, f32[5,2048]{1,0:T(8,128)}, f32[5,2,256]{2,1,0:T(2,128)}, f32[3,32]{1,0:T(4,128)}, f32[2048]{0:T(1024)}) async-done(((f32[4096]{0:T(1024)}, f32[5,2048]{1,0:T(8,128)}, f32[5,2,256]{2,1,0:T(2,128)}, f32[3,32]{1,0:T(4,128)}, f32[2048]{0:T(1024)}), (f32[4096]{0:T(1024)}, f32[5,2048]{1,0:T(8,128)}, f32[5,2,256]{2,1,0:T(2,128)}, f32[3,32]{1,0:T(4,128)}, ...) | async-done | bytes 76176 | tf_op jit(solution)/shard_map/psum | solution.py:321
  (534 shorter events, 379.7 us)
Async XLA Ops:
  7.2 35.9 copy-start.80
  7.2 82.1 %all-gather.8.cloned.1.call-start = ((), (), s32[]{:S(2)}) async-start(), calls=%async_computation.2 | async-start | bytes 4718592 | tf_op jit(solution)/shard_map/all_gather | solution.py:191
  7.9 39.5 copy-start.59
  8.0 718.8 %all-gather.6.cloned.1.call-start = ((), (), s32[]{:S(2)}) async-start(), calls=%async_computation.1 | async-start | bytes 37748736 | tf_op jit(solution)/shard_map/all_gather | solution.py:190
  8.7 1483.5 %all-gather.10.cloned.1.call-start = ((), (), s32[]{:S(2)}) async-start(), calls=%async_computation.3 | async-start | bytes 5242880 | tf_op jit(solution)/shard_map/all_gather | solution.py:44
  8.8 38.6 copy-start.20
  47.4 702.6 %copy-start.73 = (f32[512]{0:T(512)}, f32[512]{0:T(512)S(1)}, u32[]{:S(2)}) copy-start(f32[512]{0:T(512)S(1)} %get-tuple-element.1004) | copy-start | bytes 6148
  50.5 728.7 %copy-start.51 = (f32[2560]{0:T(1024)}, f32[2560]{0:T(1024)S(1)}, u32[]{:S(2)}) copy-start(f32[2560]{0:T(1024)S(1)} %get-tuple-element.881) | copy-start | bytes 30724
  50.5 728.7 %copy-start.53 = (f32[2560]{0:T(1024)}, f32[2560]{0:T(1024)S(1)}, u32[]{:S(2)}) copy-start(f32[2560]{0:T(1024)S(1)} %get-tuple-element.882) | copy-start | bytes 30724
  50.5 728.7 %copy-start.55 = (f32[2560]{0:T(1024)}, f32[2560]{0:T(1024)S(1)}, u32[]{:S(2)}) copy-start(f32[2560]{0:T(1024)S(1)} %get-tuple-element.883) | copy-start | bytes 30724
  50.5 728.7 %copy-start.57 = (f32[2560]{0:T(1024)}, f32[2560]{0:T(1024)S(1)}, u32[]{:S(2)}) copy-start(f32[2560]{0:T(1024)S(1)} %get-tuple-element.884) | copy-start | bytes 30724
  773.5 4.9 collective-permute-start
  850.5 600.2 %copy-start.38 = (f32[2,1,256,32]{2,0,3,1:T(2,128)}, f32[2,1,256,32]{2,0,3,1:T(2,128)S(1)}, u32[]{:S(2)}) copy-start(f32[2,1,256,32]{2,0,3,1:T(2,128)S(1)} %get-tuple-element.1475) | copy-start | bytes 196612
  851.5 651.5 %all-gather.12.cloned.1.call-start = ((), (), s32[]{:S(2)}) async-start(), calls=%async_computation.4 | async-start | bytes 18874368 | tf_op jit(solution)/shard_map/all_gather | solution.py:241
  852.1 813.3 %all-gather.14.cloned.1.call-start = ((), (), s32[]{:S(2)}) async-start(), calls=%async_computation.5 | async-start | bytes 5242880 | tf_op jit(solution)/shard_map/all_gather | solution.py:44
  852.1 88.3 %collective-permute-start.1 = (bf16[512,2048]{1,0:T(8,128)(2,1)}, bf16[512,2048]{1,0:T(8,128)(2,1)S(1)}, u32[]{:S(2)}, u32[]{:S(2)}) collective-permute-start(bf16[512,2048]{1,0:T(8,128)(2,1)} %param.28), channel_id=1, source_target_pairs={{0,4},{4,8},{8,12},{12,16},{16,20},{20,24},{24,28},{28,0},{1,5},{5... | collective-permute-start | bytes 6291464 | tf_op jit(solution)/shard_map/ppermute | solution.py:22
  854.9 160.7 %collective-permute-start.2 = (bf16[512,2048]{1,0:T(8,128)(2,1)}, bf16[512,2048]{1,0:T(8,128)(2,1)}, u32[]{:S(2)}, u32[]{:S(2)}) collective-permute-start(bf16[512,2048]{1,0:T(8,128)(2,1)} %param.28), channel_id=1, source_target_pairs={{0,28},{4,0},{8,4},{12,8},{16,12},{20,16},{24,20},{28,24},{1,29},{... | collective-permute-start | bytes 6291464 | tf_op jit(solution)/shard_map/ppermute | solution.py:27
  941.8 162.3 %collective-permute-start.3 = (bf16[512,2048]{1,0:T(8,128)(2,1)S(1)}, bf16[512,2048]{1,0:T(8,128)(2,1)}, u32[]{:S(2)}, u32[]{:S(2)}) collective-permute-start(bf16[512,2048]{1,0:T(8,128)(2,1)S(1)} %collective-permute-done.1), channel_id=1, source_target_pairs={{0,4},{4,8},{8,12},{12,16},{16,20},{20,24},{24,28},{28,0},{1,5},{5... | collective-permute-start | bytes 6291464 | tf_op jit(solution)/shard_map/ppermute | solution.py:22
  1015.6 173.2 %collective-permute-start.4 = (bf16[512,2048]{1,0:T(8,128)(2,1)}, bf16[512,2048]{1,0:T(8,128)(2,1)}, u32[]{:S(2)}, u32[]{:S(2)}) collective-permute-start(bf16[512,2048]{1,0:T(8,128)(2,1)} %collective-permute-done.2), channel_id=1, source_target_pairs={{0,28},{4,0},{8,4},{12,8},{16,12},{20,16},{24,20},{28,24},{1,29},{... | collective-permute-start | bytes 6291464 | tf_op jit(solution)/shard_map/ppermute | solution.py:27
  1104.1 164.9 %collective-permute-start.5 = (bf16[512,2048]{1,0:T(8,128)(2,1)}, bf16[512,2048]{1,0:T(8,128)(2,1)}, u32[]{:S(2)}, u32[]{:S(2)}) collective-permute-start(bf16[512,2048]{1,0:T(8,128)(2,1)} %collective-permute-done.3), channel_id=1, source_target_pairs={{0,4},{4,8},{8,12},{12,16},{16,20},{20,24},{24,28},{28,0},{1,5},{5... | collective-permute-start | bytes 6291464 | tf_op jit(solution)/shard_map/ppermute | solution.py:22
  1176.9 326.0 %copy-start.71 = (f32[2048]{0:T(1024)}, f32[2048]{0:T(1024)S(1)}, u32[]{:S(2)}) copy-start(f32[2048]{0:T(1024)S(1)} %mul.967) | copy-start | bytes 24580
  1188.8 278.4 %collective-permute-start.6 = (bf16[512,2048]{1,0:T(8,128)(2,1)}, bf16[512,2048]{1,0:T(8,128)(2,1)}, u32[]{:S(2)}, u32[]{:S(2)}) collective-permute-start(bf16[512,2048]{1,0:T(8,128)(2,1)} %collective-permute-done.4), channel_id=1, source_target_pairs={{0,28},{4,0},{8,4},{12,8},{16,12},{20,16},{24,20},{28,24},{1,29},{... | collective-permute-start | bytes 6291464 | tf_op jit(solution)/shard_map/ppermute | solution.py:27
  1269.0 201.4 %collective-permute-start.7 = (bf16[512,2048]{1,0:T(8,128)(2,1)}, bf16[512,2048]{1,0:T(8,128)(2,1)S(1)}, u32[]{:S(2)}, u32[]{:S(2)}) collective-permute-start(bf16[512,2048]{1,0:T(8,128)(2,1)} %collective-permute-done.5), channel_id=1, source_target_pairs={{0,4},{4,8},{8,12},{12,16},{16,20},{20,24},{24,28},{28,0},{1,5},{5... | collective-permute-start | bytes 6291464 | tf_op jit(solution)/shard_map/ppermute | solution.py:22
  1552.7 10.3 slice-start.2
  1554.8 8.3 slice-start.3
  1581.7 651.5 %all-reduce.25.cloned.1.call-start = ((), (), s32[]{:S(2)}) async-start(), calls=%async_computation.8 | async-start | bytes 33554432 | tf_op jit(solution)/shard_map/psum | solution.py:234
  1609.2 12.2 copy-start.35
  1712.2 14.5 copy-start.6
  1712.2 14.5 copy-start.23
  1712.3 15.7 copy-start.44
  1732.3 9.8 copy-start.33
  1735.0 8.5 copy-start
  1792.5 14.5 copy-start.6
  1792.5 14.5 copy-start.23
  1792.5 15.7 copy-start.44
  1812.6 9.8 copy-start.33
  1815.2 8.5 copy-start
  1861.4 12.6 slice-start
  1874.1 8.6 copy-start.52
  1874.1 8.6 copy-start.54
  1874.1 8.6 copy-start.56
  1874.1 8.6 copy-start.58
  1894.4 9.5 collective-permute-start.8
  1904.1 8.5 copy-start.30
  1912.7 22.9 copy-start.48
  1946.0 1963.4 %reduce-scatter.2.cloned.1.call-start = ((), (), s32[]{:S(2)}) async-start(), calls=%async_computation.6 | async-start | bytes 123273216 | tf_op jit(solution)/shard_map/reduce_scatter | solution.py:298
  1946.7 30.2 copy-start.22
  2059.7 1924.8 %all-reduce.23.cloned.1.call-start = ((), (), s32[]{:S(2)}) async-start(), calls=%async_computation.7 | async-start | bytes 204800 | tf_op jit(solution)/shard_map/psum | solution.py:321
  (75 other events, 241.0 us)
Sparse Core Ops, SparseCore 0:
  10.2 79.0 all-gather.7
  90.8 635.9 all-gather.5
  851.6 152.1 all-gather.9
  1005.8 431.4 all-gather.11
  1581.8 83.4 all-gather.13
  1946.2 287.0 all-reduce.24
  2237.1 1672.3 reduce-scatter.1
  3915.0 69.3 all-reduce.22
